TPU v7x, 32 devices: a whole 2x2x4 slice. The times are simulated.
32 devices in a mesh: day: 2 (over y), stu: 16 (over z, x, core).
Axes of the slice: x: 2, y: 2, z: 4, core: 2. Of those that a mesh axis runs over, the one named last changes fastest.
Arguments:
- performance: bfloat16 [64, 128, 1024], P('day', 'stu'), may hold values from -8 to 8
- student_factor: bfloat16 [128, 256], P('stu'), may hold values from -0.5 to 0.5
- skill_factor: bfloat16 [1024, 256], replicated, may hold values from -0.1875 to 0.1875
- day_prev: float32 [64, 256], P('day'), may hold values from -6 to 6
- ar_coef: float32 [7], replicated, may hold values from -0.3 to 0.3
Outputs:
- day_factor: float32 [64, 256], P('day', 'stu')
- residual: float32 [64, 256], P('day', 'stu')
All inputs are finite; a program needn't handle non-finite values.
Results may differ from a plain program's by a relative error of at most 0.0003.
Values sent between devices are 32-bit elements; how exact they have to be, the bound alone decides.
No kernel may reach another device: no remote copies, remote signals or barrier semaphores. Data moves between devices by JAX's collectives and lax.ppermute only.
A program may use at most 64 MiB of HBM per device.

v0:
```python
import jax
import jax.numpy as jnp
from jax import lax
from jax.sharding import PartitionSpec as P

LAGS = 7
ITERS = 3
smoothing = 1.0


def shifted(block, axis, distance):
    devices = range(lax.axis_size(axis))
    route = [(i - distance, i) for i in devices if i - distance in devices]
    return lax.ppermute(block, axis, route)


def filter_rows(extended, coef, count):
    out = extended[LAGS : LAGS + count]
    for lag in range(1, LAGS + 1):
        out = out - coef[lag - 1] * extended[LAGS - lag : LAGS - lag + count]
    return out


def smooth(values, coef):
    count = values.shape[0]
    below = shifted(values[count - LAGS :], "day", 1)
    ahead_core = filter_rows(jnp.concatenate([below, values], 0), coef, count)
    above = shifted(ahead_core[:LAGS], "day", -1)
    ahead = jnp.concatenate([ahead_core, above], 0)
    out = ahead[:count]
    for lag in range(1, LAGS + 1):
        out = out - coef[lag - 1] * ahead[lag : lag + count]
    return out


def with_gram(values, gram_part):
    return jnp.dot(
        lax.all_gather(values, "stu", axis=1, tiled=True),
        gram_part,
        precision=lax.Precision.HIGHEST,
        preferred_element_type=jnp.float32,
    )


def operate(values, gram_part, coef):
    return with_gram(values, gram_part) + smoothing * smooth(values, coef)


def global_total(value):
    return lax.psum(value, ("day", "stu"))


def summed_gram(local_gram):
    return lax.psum(local_gram, "stu")


def local(performance, student_factor, skill_factor, day_prev, ar_coef):
    days, students, skills = performance.shape
    rank = skill_factor.shape[1]
    proj = jnp.dot(
        performance.reshape(days * students, skills),
        skill_factor,
        preferred_element_type=jnp.float32,
    )
    proj = proj.reshape(days, students, rank)
    local_terms = jnp.sum(proj * student_factor.astype(jnp.float32)[None], axis=1)
    local_gram = jnp.dot(student_factor.T, student_factor, preferred_element_type=jnp.float32)
    skill_gram = jnp.dot(skill_factor.T, skill_factor, preferred_element_type=jnp.float32)
    columns = rank // lax.axis_size("stu")
    first_col = lax.axis_index("stu") * columns
    gram = summed_gram(local_gram) * skill_gram
    mttkrp = lax.psum_scatter(local_terms, "stu", scatter_dimension=1, tiled=True)
    gram_part = lax.dynamic_slice_in_dim(gram, first_col, columns, 1)
    day_factor = lax.dynamic_slice_in_dim(day_prev, first_col, columns, 1)
    residual = mttkrp - operate(day_factor, gram_part, ar_coef)
    direction = residual
    norm_now = global_total(jnp.sum(residual * residual))
    for step in range(ITERS):
        image = operate(direction, gram_part, ar_coef)
        alpha = norm_now / global_total(jnp.sum(direction * image))
        day_factor = day_factor + alpha * direction
        residual = residual - alpha * image
        norm_next = global_total(jnp.sum(residual * residual))
        direction = residual + norm_next / norm_now * direction
        norm_now = norm_next
    return (day_factor, residual)


def solution(mesh):
    return jax.shard_map(
        local,
        mesh=mesh,
        in_specs=(P("day", "stu", None), P("stu", None), P(), P("day", None), P()),
        out_specs=(P("day", "stu"), P("day", "stu")),
        check_vma=False,
    )
```

profile of v0, /device:TPU:14, one launch (start us, length us, event | category | flops | bytes accessed | tf_op | source)
XLA Modules:
  0.0 491.8 jit_solution(908321572501885240)
XLA Ops:
  7.2 0.9 constant_dynamic-slice_fusion
  8.1 0.1 copy.10
  8.2 0.1 slice.333
  8.3 1.3 collective-permute-start
  9.6 1.7 fusion.139
  11.3 0.0 reduce-scatter.2.cloned.1.call-start
  11.3 0.6 copy-done.2
  11.9 0.3 fusion
  12.3 0.8 copy.9
  13.1 0.3 fusion.140
  13.4 0.3 copy-done.3
  13.7 0.7 fusion.138
  14.3 15.5 %all_gather.12 = f32[32,256]{0,1:T(8,128)S(1)} all-gather(f32[32,16]{0,1:T(8,128)S(1)} %copy.10), channel_id=1, replica_groups=mesh['day'=2,'stu'=16] {'stu'}, dimensions={1}, use_global_device_ids=true | all-gather | bytes 34816 | tf_op jit(solution)/shard_map/all_gather | solution.py:38
  29.8 4.5 fusion.120
  34.3 4.6 collective-permute-start.1
  38.9 64.2 %all-reduce.3.cloned.1.call-done = f32[256,256]{0,1:T(8,128)} async-done(((f32[256,256]{0,1:T(8,128)}), f32[256,256]{0,1:T(8,128)}) %all-reduce.3.cloned.1.call-update) | async-done | bytes 262160 | tf_op jit(solution)/shard_map/psum | solution.py:54
  103.1 0.7 dynamic-slice_multiply_fusion
  103.8 57.7 %reduce-scatter.2.cloned.1.call-done = f32[32,16]{0,1:T(8,128)} async-done(((f32[32,256]{0,1:T(8,128)}), f32[32,16]{0,1:T(8,128)}) %reduce-scatter.2.cloned.1.call-update) | async-done | bytes 2064 | tf_op jit(solution)/shard_map/reduce_scatter | solution.py:72
  161.5 5.2 %fusion.104 = f32[32,16]{0,1:T(8,128)S(1)} fusion(f32[32,16]{0,1:T(8,128)} %reduce-scatter.2.cloned.1.call-done, f32[7,16]{0,1:T(8,128)S(1)} %collective-permute-done.1, f32[32,16]{0,1:T(8,128)S(1)} %fusion.120, f32[]{:T(128)} %bitcast.7, f32[]{:T(128)} %bitcast.6, f32[]{:T(128)} %bitcast.5, f32[]{:T(128)} %bitcast.4, f32[]{:T(128)} %bitcast.3, ...), kind=kOutput, calls=%fused_computation.173 | convolution fusion | flops 1584640 | bytes 55772 | tf_op jit(solution)/shard_map/dot_general | solution.py:37
  166.7 0.1 slice.359
  166.8 1.3 collective-permute-start.2
  168.1 4.2 collective-permute-done.2
  172.3 4.5 fusion.86
  176.8 1.6 collective-permute-start.3
  178.5 15.4 %all_gather.13 = f32[32,256]{0,1:T(8,128)S(1)} all-gather(f32[32,16]{0,1:T(8,128)S(1)} %fusion.104), channel_id=1, replica_groups=mesh['day'=2,'stu'=16] {'stu'}, dimensions={1}, use_global_device_ids=true | all-gather | bytes 34816 | tf_op jit(solution)/shard_map/all_gather | solution.py:38
  193.8 5.2 %multiply_reduce_fusion.4 = (f32[]{:T(128)}, f32[]{:T(128)}, f32[32,16]{0,1:T(8,128)S(1)}) fusion(f32[32,16]{0,1:T(8,128)S(1)} %fusion.104, f32[7,16]{0,1:T(8,128)S(1)} %collective-permute-done.3, f32[32,16]{0,1:T(8,128)S(1)} %fusion.86, f32[]{:T(128)} %bitcast.7, f32[]{:T(128)} %bitcast.6, f32[]{:T(128)} %bitcast.5, f32[]{:T(128)} %bitcast.4, ...), kind=kOutput, calls=%fused_computation.235 | convolution fusion | flops 1586174 | bytes 55780 | tf_op jit(solution)/shard_map/dot_general | solution.py:37
  199.0 44.1 %all-reduce = (f32[]{:T(128)}, f32[]{:T(128)}) all-reduce(f32[]{:T(128)} %get-tuple-element.3, f32[]{:T(128)} %get-tuple-element.2), channel_id=1, replica_groups=mesh['day'=2,'stu'=16] {'day','stu'}, use_global_device_ids=true, to_apply=%region_4.0 | all-reduce | flops 2 | bytes 16 | tf_op jit(solution)/shard_map/psum | solution.py:50
  244.4 0.6 multiply_reduce_fusion.3
  245.1 38.6 %psum.52 = f32[]{:T(128)} all-reduce(f32[]{:T(128)} %multiply_reduce_fusion.3), channel_id=1, replica_groups=mesh['day'=2,'stu'=16] {'day','stu'}, use_global_device_ids=true, to_apply=%region_8.0 | all-reduce | flops 1 | bytes 8 | tf_op jit(solution)/shard_map/psum | solution.py:50
  285.1 0.1 slice.385
  285.1 1.3 collective-permute-start.4
  286.4 4.2 collective-permute-done.4
  290.7 4.5 fusion.53
  295.1 1.6 collective-permute-start.5
  296.8 18.0 %all_gather.14 = f32[32,256]{0,1:T(8,128)S(1)} all-gather(f32[32,16]{0,1:T(8,128)S(1)} %multiply_add_fusion.2), channel_id=1, replica_groups=mesh['day'=2,'stu'=16] {'stu'}, dimensions={1}, use_global_device_ids=true | all-gather | bytes 34816 | tf_op jit(solution)/shard_map/all_gather | solution.py:38
  314.8 5.2 %multiply_reduce_fusion.2 = (f32[]{:T(128)}, f32[32,16]{0,1:T(8,128)S(1)}) fusion(f32[32,16]{0,1:T(8,128)S(1)} %multiply_add_fusion.2, f32[7,16]{0,1:T(8,128)S(1)} %collective-permute-done.5, f32[32,16]{0,1:T(8,128)S(1)} %fusion.53, f32[]{:T(128)} %bitcast.7, f32[]{:T(128)} %bitcast.6, f32[]{:T(128)} %bitcast.5, f32[]{:T(128)} %bitcast.4, f32[]{:T(128)} %bitcast.3, ...), kind=kOutput, calls=%fused_computation.231 | convolution fusion | flops 1585151 | bytes 55776 | tf_op jit(solution)/shard_map/dot_general | solution.py:37
  320.0 43.0 %psum.53 = f32[]{:T(128)} all-reduce(f32[]{:T(128)} %get-tuple-element.10), channel_id=1, replica_groups=mesh['day'=2,'stu'=16] {'day','stu'}, use_global_device_ids=true, to_apply=%region_10.0 | all-reduce | flops 1 | bytes 8 | tf_op jit(solution)/shard_map/psum | solution.py:50
  364.2 0.6 multiply_reduce_fusion.1
  364.8 39.0 %psum.54 = f32[]{:T(128)} all-reduce(f32[]{:T(128)} %get-tuple-element.8), channel_id=1, replica_groups=mesh['day'=2,'stu'=16] {'day','stu'}, use_global_device_ids=true, to_apply=%region_12.0 | all-reduce | flops 1 | bytes 8 | tf_op jit(solution)/shard_map/psum | solution.py:50
  405.2 0.1 slice.411
  405.3 1.3 collective-permute-start.6
  406.5 4.2 collective-permute-done.6
  410.8 4.5 fusion.20
  415.3 1.6 collective-permute-start.7
  416.9 17.6 %all_gather.15 = f32[32,256]{0,1:T(8,128)S(1)} all-gather(f32[32,16]{0,1:T(8,128)S(1)} %multiply_add_fusion.1), channel_id=1, replica_groups=mesh['day'=2,'stu'=16] {'stu'}, dimensions={1}, use_global_device_ids=true | all-gather | bytes 34816 | tf_op jit(solution)/shard_map/all_gather | solution.py:38
  434.5 5.1 %multiply_reduce_fusion = (f32[]{:T(128)}, f32[32,16]{0,1:T(8,128)S(1)}) fusion(f32[32,16]{0,1:T(8,128)S(1)} %multiply_add_fusion.1, f32[7,16]{0,1:T(8,128)S(1)} %collective-permute-done.7, f32[32,16]{0,1:T(8,128)S(1)} %fusion.20, f32[]{:T(128)} %bitcast.7, f32[]{:T(128)} %bitcast.6, f32[]{:T(128)} %bitcast.5, f32[]{:T(128)} %bitcast.4, f32[]{:T(128)} %bitcast.3, ...), kind=kOutput, calls=%fused_computation.227 | convolution fusion | flops 1585151 | bytes 55776 | tf_op jit(solution)/shard_map/dot_general | solution.py:37
  439.7 43.2 %psum.55 = f32[]{:T(128)} all-reduce(f32[]{:T(128)} %get-tuple-element.6), channel_id=1, replica_groups=mesh['day'=2,'stu'=16] {'day','stu'}, use_global_device_ids=true, to_apply=%region_14.0 | all-reduce | flops 1 | bytes 8 | tf_op jit(solution)/shard_map/psum | solution.py:50
  484.3 0.6 multiply_subtract_fusion
  (17 shorter events, 0.1 us)
Async XLA Ops:
  7.2 4.8 copy-start
  7.2 4.8 copy-start.1
  7.2 95.9 %all-reduce.3.cloned.1.call-start = ((), (), s32[]{:S(2)}) async-start(), calls=%async_computation.2 | async-start | bytes 524288 | tf_op jit(solution)/shard_map/psum | solution.py:54
  8.3 21.6 %collective-permute-start = (f32[7,16]{0,1:T(8,128)S(1)}, f32[7,16]{0,1:T(8,128)S(1)}, u32[]{:S(2)}, u32[]{:S(2)}) collective-permute-start(f32[7,16]{0,1:T(8,128)S(1)} %slice.333), channel_id=1, source_target_pairs={{0,16},{1,17},{2,18},{3,19},{4,20},{5,21},{6,22},{7,23},{8,24},{9,... | collective-permute-start | bytes 1352 | tf_op jit(solution)/shard_map/ppermute | solution.py:14
  11.2 0.7 copy-start.2
  11.3 150.2 %reduce-scatter.2.cloned.1.call-start = ((), (), s32[]{:S(2)}) async-start(), calls=%async_computation.1 | async-start | bytes 139264 | tf_op jit(solution)/shard_map/reduce_scatter | solution.py:72
  13.0 0.7 copy-start.3
  34.3 69.5 %collective-permute-start.1 = (f32[7,16]{0,1:T(8,128)S(1)}, f32[7,16]{0,1:T(8,128)S(1)}, u32[]{:S(2)}, u32[]{:S(2)}) collective-permute-start(f32[7,16]{0,1:T(8,128)S(1)} %bitcast.27), channel_id=1, source_target_pairs={{16,0},{17,1},{18,2},{19,3},{20,4},{21,5},{22,6},{23,7},{24,8},{25... | collective-permute-start | bytes 1352 | tf_op jit(solution)/shard_map/ppermute | solution.py:14
  166.8 5.5 %collective-permute-start.2 = (f32[7,16]{0,1:T(8,128)S(1)}, f32[7,16]{0,1:T(8,128)S(1)}, u32[]{:S(2)}, u32[]{:S(2)}) collective-permute-start(f32[7,16]{0,1:T(8,128)S(1)} %slice.359), channel_id=1, source_target_pairs={{0,16},{1,17},{2,18},{3,19},{4,20},{5,21},{6,22},{7,23},{8,24},{9,... | collective-permute-start | bytes 1352 | tf_op jit(solution)/shard_map/ppermute | solution.py:14
  176.8 17.0 %collective-permute-start.3 = (f32[7,16]{0,1:T(8,128)S(1)}, f32[7,16]{0,1:T(8,128)S(1)}, u32[]{:S(2)}, u32[]{:S(2)}) collective-permute-start(f32[7,16]{0,1:T(8,128)S(1)} %bitcast.29), channel_id=1, source_target_pairs={{16,0},{17,1},{18,2},{19,3},{20,4},{21,5},{22,6},{23,7},{24,8},{25... | collective-permute-start | bytes 1352 | tf_op jit(solution)/shard_map/ppermute | solution.py:14
  285.1 5.5 %collective-permute-start.4 = (f32[7,16]{0,1:T(8,128)S(1)}, f32[7,16]{0,1:T(8,128)S(1)}, u32[]{:S(2)}, u32[]{:S(2)}) collective-permute-start(f32[7,16]{0,1:T(8,128)S(1)} %slice.385), channel_id=1, source_target_pairs={{0,16},{1,17},{2,18},{3,19},{4,20},{5,21},{6,22},{7,23},{8,24},{9,... | collective-permute-start | bytes 1352 | tf_op jit(solution)/shard_map/ppermute | solution.py:14
  295.1 19.6 %collective-permute-start.5 = (f32[7,16]{0,1:T(8,128)S(1)}, f32[7,16]{0,1:T(8,128)S(1)}, u32[]{:S(2)}, u32[]{:S(2)}) collective-permute-start(f32[7,16]{0,1:T(8,128)S(1)} %bitcast.30), channel_id=1, source_target_pairs={{16,0},{17,1},{18,2},{19,3},{20,4},{21,5},{22,6},{23,7},{24,8},{25... | collective-permute-start | bytes 1352 | tf_op jit(solution)/shard_map/ppermute | solution.py:14
  405.3 5.5 %collective-permute-start.6 = (f32[7,16]{0,1:T(8,128)S(1)}, f32[7,16]{0,1:T(8,128)S(1)}, u32[]{:S(2)}, u32[]{:S(2)}) collective-permute-start(f32[7,16]{0,1:T(8,128)S(1)} %slice.411), channel_id=1, source_target_pairs={{0,16},{1,17},{2,18},{3,19},{4,20},{5,21},{6,22},{7,23},{8,24},{9,... | collective-permute-start | bytes 1352 | tf_op jit(solution)/shard_map/ppermute | solution.py:14
  415.3 19.3 %collective-permute-start.7 = (f32[7,16]{0,1:T(8,128)S(1)}, f32[7,16]{0,1:T(8,128)S(1)}, u32[]{:S(2)}, u32[]{:S(2)}) collective-permute-start(f32[7,16]{0,1:T(8,128)S(1)} %bitcast.28), channel_id=1, source_target_pairs={{16,0},{17,1},{18,2},{19,3},{20,4},{21,5},{22,6},{23,7},{24,8},{25... | collective-permute-start | bytes 1352 | tf_op jit(solution)/shard_map/ppermute | solution.py:14
Sparse Core Ops, SparseCore 0:
  11.4 91.6 all-reduce.2
  106.5 54.8 reduce-scatter.1
where the time goes:
time: 494 us; the launch traced here: 492 us
  blocking collectives  274 us (55%)
  waiting for transfers between devices  135 us (27%)
  matrix products  23.1 us (5%)
  between operations  20.9 us (4%)
  other arithmetic  20.4 us (4%)
  starting transfers between devices  14.7 us (3%)
    psum x5, blocking collectives, global_total(): return lax.psum(value, ('day', 'stu'))  208 us
    all_gather x4, blocking collectives, with_gram(): lax.all_gather(values, 'stu', axis=1, tiled=True)  66.5 us
    psum x1, waiting for transfers between devices, summed_gram(): return lax.psum(local_gram, 'stu')  64.2 us
    reduce_scatter x1, waiting for transfers between devices, local(): lax.psum_scatter(local_terms, 'stu', scatter_dimension=1, tiled=True)  57.7 us
    dot_general x4, matrix products, with_gram(): jnp.dot(lax.all_gather(values, 'stu', axis=1, tiled=True), gram_part, pre...  20.8 us
    sub x4, other arithmetic, filter_rows(): out = out - coef[lag - 1] * extended[LAGS - lag:LAGS - lag + count]  17.8 us
    ppermute x8, starting transfers between devices, shifted(): return lax.ppermute(block, axis, route)  14.6 us
    ppermute x8, waiting for transfers between devices, shifted(): return lax.ppermute(block, axis, route)  12.7 us
  transfers between devices with their start and end apart: 10, of which 5 were waited for; matrix products, arithmetic and copies ran while one was open for 2% of the time, Pallas kernels for 0%

commit v1 on v0

--- a/solution.py
+++ b/solution.py
@@ -51,7 +51,7 @@
 
 
 def summed_gram(local_gram):
-    return lax.psum(local_gram, "stu")
+    return jnp.sum(lax.all_gather(local_gram, "stu"), axis=0)
 
 
 def local(performance, student_factor, skill_factor, day_prev, ar_coef):

time: 494 us -> 452 us (0.915)
  waiting for transfers between devices: 135 us -> 88.6 us
    psum x1 -> x0, waiting for transfers between devices: 64.2 us -> none  [summed_gram(): return lax.psum(local_gram, 'stu')]
    all_gather x0 -> x1, waiting for transfers between devices: none -> 20.6 us  [summed_gram(): return jnp.sum(lax.all_gather(local_gram, 'stu'), axis=0)]
  transfers between devices with their start and end apart: 10 -> 10, of which waited for: 5 -> 5; matrix products, arithmetic and copies ran while one was open for 2% -> 3% of each run, Pallas kernels for 0% -> 0%
where the time goes in v1:
time: 452 us; the launch traced here: 450 us
  blocking collectives  274 us (61%)
  waiting for transfers between devices  88.6 us (20%)
  matrix products  24.6 us (5%)
  other arithmetic  23.3 us (5%)
  between operations  20.9 us (5%)
  starting transfers between devices  14.7 us (3%)
    psum x5, blocking collectives, global_total(): return lax.psum(value, ('day', 'stu'))  208 us
    all_gather x4, blocking collectives, with_gram(): lax.all_gather(values, 'stu', axis=1, tiled=True)  66.6 us
    reduce_scatter x1, waiting for transfers between devices, local(): lax.psum_scatter(local_terms, 'stu', scatter_dimension=1, tiled=True)  55.2 us
    dot_general x4, matrix products, with_gram(): jnp.dot(lax.all_gather(values, 'stu', axis=1, tiled=True), gram_part, pre...  21.2 us
    all_gather x1, waiting for transfers between devices, summed_gram(): return jnp.sum(lax.all_gather(local_gram, 'stu'), axis=0)  20.6 us
    sub x4, other arithmetic, filter_rows(): out = out - coef[lag - 1] * extended[LAGS - lag:LAGS - lag + count]  18.3 us
    ppermute x8, starting transfers between devices, shifted(): return lax.ppermute(block, axis, route)  14.6 us
    ppermute x8, waiting for transfers between devices, shifted(): return lax.ppermute(block, axis, route)  12.8 us
  transfers between devices with their start and end apart: 10, of which 5 were waited for; matrix products, arithmetic and copies ran while one was open for 3% of the time, Pallas kernels for 0%

profile of v1, /device:TPU:14, one launch (start us, length us, event | category | flops | bytes accessed | tf_op | source)
XLA Modules:
  0.0 450.1 jit_solution(7622981522461853916)
XLA Ops:
  7.2 1.7 fusion.139
  9.0 0.8 constant_dynamic-slice_fusion.1
  9.8 0.1 copy.11
  9.8 0.1 slice.333
  9.9 1.3 collective-permute-start
  11.2 0.7 convert_element_type.3
  11.9 1.4 fusion
  13.3 0.8 copy.9
  14.1 0.3 fusion.140
  14.4 1.6 fusion.138
  16.0 15.6 %all_gather.18 = f32[32,256]{0,1:T(8,128)S(1)} all-gather(f32[32,16]{0,1:T(8,128)S(1)} %copy.11), channel_id=1, replica_groups=mesh['day'=2,'stu'=16] {'stu'}, dimensions={1}, use_global_device_ids=true | all-gather | bytes 34816 | tf_op jit(solution)/shard_map/all_gather | solution.py:38
  31.6 4.6 %fusion.120 = f32[32,16]{0,1:T(8,128)S(1)} fusion(f32[32,16]{0,1:T(8,128)S(1)} %copy.11, f32[7,16]{0,1:T(8,128)S(1)} %collective-permute-done, f32[]{:T(128)} %bitcast.8, f32[]{:T(128)} %bitcast.7, f32[]{:T(128)} %bitcast.6, f32[]{:T(128)} %bitcast.5, f32[]{:T(128)} %bitcast.4, f32[]{:T(128)} %bitcast.3, f32[]{:T(128)} %bitcast.2), kind=kLoop, calls=%fused_computation.200 | loop fusion | flops 10752 | bytes 4572 | tf_op jit(solution)/shard_map/sub | solution.py:20
  36.2 4.5 collective-permute-start.1
  40.7 20.6 %all-gather.3.cloned.1.call-done = f32[4096,256]{1,0:T(8,128)} async-done(((f32[256,256]{1,0:T(8,128)}), f32[4096,256]{1,0:T(8,128)}) %all-gather.3.cloned.1.call-update) | async-done | bytes 4194320 | tf_op jit(solution)/shard_map/all_gather | solution.py:54
  61.3 2.5 reduce_sum.73
  63.7 0.1 constant_dynamic-slice_fusion
  63.9 0.1 copy.12
  63.9 55.2 %reduce-scatter.2.cloned.1.call-done = f32[32,16]{0,1:T(8,128)} async-done(((f32[32,256]{0,1:T(8,128)}), f32[32,16]{0,1:T(8,128)}) %reduce-scatter.2.cloned.1.call-update) | async-done | bytes 2064 | tf_op jit(solution)/shard_map/reduce_scatter | solution.py:72
  119.2 5.3 %fusion.104 = f32[32,16]{0,1:T(8,128)S(1)} fusion(f32[32,16]{0,1:T(8,128)} %reduce-scatter.2.cloned.1.call-done, f32[7,16]{0,1:T(8,128)S(1)} %collective-permute-done.1, f32[32,16]{0,1:T(8,128)S(1)} %fusion.120, f32[]{:T(128)} %bitcast.8, f32[]{:T(128)} %bitcast.7, f32[]{:T(128)} %bitcast.6, f32[]{:T(128)} %bitcast.5, f32[]{:T(128)} %bitcast.4, ...), kind=kOutput, calls=%fused_computation.173 | convolution fusion | flops 1584640 | bytes 55772 | tf_op jit(solution)/shard_map/dot_general | solution.py:37
  124.5 0.1 slice.359
  124.6 1.3 collective-permute-start.2
  125.9 4.2 collective-permute-done.2
  130.1 4.6 %fusion.86 = f32[32,16]{0,1:T(8,128)S(1)} fusion(f32[32,16]{0,1:T(8,128)S(1)} %fusion.104, f32[7,16]{0,1:T(8,128)S(1)} %collective-permute-done.2, f32[]{:T(128)} %bitcast.8, f32[]{:T(128)} %bitcast.7, f32[]{:T(128)} %bitcast.6, f32[]{:T(128)} %bitcast.5, f32[]{:T(128)} %bitcast.4, f32[]{:T(128)} %bitcast.3, f32[]{:T(128)} %bitcast.2), kind=kLoop, calls=%fused_computation.144 | loop fusion | flops 10752 | bytes 4572 | tf_op jit(solution)/shard_map/sub | solution.py:20
  134.7 1.6 collective-permute-start.3
  136.4 15.4 %all_gather.21 = f32[32,256]{0,1:T(8,128)S(1)} all-gather(f32[32,16]{0,1:T(8,128)S(1)} %fusion.104), channel_id=1, replica_groups=mesh['day'=2,'stu'=16] {'stu'}, dimensions={1}, use_global_device_ids=true | all-gather | bytes 34816 | tf_op jit(solution)/shard_map/all_gather | solution.py:38
  151.7 5.3 %multiply_reduce_fusion.4 = (f32[]{:T(128)}, f32[]{:T(128)}, f32[32,16]{0,1:T(8,128)S(1)}) fusion(f32[32,16]{0,1:T(8,128)S(1)} %fusion.104, f32[7,16]{0,1:T(8,128)S(1)} %collective-permute-done.3, f32[32,16]{0,1:T(8,128)S(1)} %fusion.86, f32[]{:T(128)} %bitcast.8, f32[]{:T(128)} %bitcast.7, f32[]{:T(128)} %bitcast.6, f32[]{:T(128)} %bitcast.5, ...), kind=kOutput, calls=%fused_computation.235 | convolution fusion | flops 1586174 | bytes 55780 | tf_op jit(solution)/shard_map/dot_general | solution.py:37
  157.0 44.0 %all-reduce = (f32[]{:T(128)}, f32[]{:T(128)}) all-reduce(f32[]{:T(128)} %get-tuple-element.3, f32[]{:T(128)} %get-tuple-element.2), channel_id=1, replica_groups=mesh['day'=2,'stu'=16] {'day','stu'}, use_global_device_ids=true, to_apply=%region_4.0 | all-reduce | flops 2 | bytes 16 | tf_op jit(solution)/shard_map/psum | solution.py:50
  202.4 0.6 multiply_reduce_fusion.3
  203.1 38.6 %psum.44 = f32[]{:T(128)} all-reduce(f32[]{:T(128)} %multiply_reduce_fusion.3), channel_id=1, replica_groups=mesh['day'=2,'stu'=16] {'day','stu'}, use_global_device_ids=true, to_apply=%region_8.0 | all-reduce | flops 1 | bytes 8 | tf_op jit(solution)/shard_map/psum | solution.py:50
  243.0 0.1 slice.385
  243.1 1.3 collective-permute-start.4
  244.4 4.2 collective-permute-done.4
  248.6 4.6 %fusion.53 = f32[32,16]{0,1:T(8,128)S(1)} fusion(f32[32,16]{0,1:T(8,128)S(1)} %multiply_add_fusion.2, f32[7,16]{0,1:T(8,128)S(1)} %collective-permute-done.4, f32[]{:T(128)} %bitcast.8, f32[]{:T(128)} %bitcast.7, f32[]{:T(128)} %bitcast.6, f32[]{:T(128)} %bitcast.5, f32[]{:T(128)} %bitcast.4, f32[]{:T(128)} %bitcast.3, f32[]{:T(128)} %bitcast.2), kind=kLoop, calls=%fused_computation.89 | loop fusion | flops 10752 | bytes 4572 | tf_op jit(solution)/shard_map/sub | solution.py:20
  253.2 1.6 collective-permute-start.5
  254.9 18.0 %all_gather.22 = f32[32,256]{0,1:T(8,128)S(1)} all-gather(f32[32,16]{0,1:T(8,128)S(1)} %multiply_add_fusion.2), channel_id=1, replica_groups=mesh['day'=2,'stu'=16] {'stu'}, dimensions={1}, use_global_device_ids=true | all-gather | bytes 34816 | tf_op jit(solution)/shard_map/all_gather | solution.py:38
  272.8 5.3 %multiply_reduce_fusion.2 = (f32[]{:T(128)}, f32[32,16]{0,1:T(8,128)S(1)}) fusion(f32[32,16]{0,1:T(8,128)S(1)} %multiply_add_fusion.2, f32[7,16]{0,1:T(8,128)S(1)} %collective-permute-done.5, f32[32,16]{0,1:T(8,128)S(1)} %fusion.53, f32[]{:T(128)} %bitcast.8, f32[]{:T(128)} %bitcast.7, f32[]{:T(128)} %bitcast.6, f32[]{:T(128)} %bitcast.5, f32[]{:T(128)} %bitcast.4, ...), kind=kOutput, calls=%fused_computation.231 | convolution fusion | flops 1585151 | bytes 55776 | tf_op jit(solution)/shard_map/dot_general | solution.py:37
  278.2 43.0 %psum.45 = f32[]{:T(128)} all-reduce(f32[]{:T(128)} %get-tuple-element.10), channel_id=1, replica_groups=mesh['day'=2,'stu'=16] {'day','stu'}, use_global_device_ids=true, to_apply=%region_10.0 | all-reduce | flops 1 | bytes 8 | tf_op jit(solution)/shard_map/psum | solution.py:50
  322.4 0.6 multiply_reduce_fusion.1
  323.0 39.0 %psum.46 = f32[]{:T(128)} all-reduce(f32[]{:T(128)} %get-tuple-element.8), channel_id=1, replica_groups=mesh['day'=2,'stu'=16] {'day','stu'}, use_global_device_ids=true, to_apply=%region_12.0 | all-reduce | flops 1 | bytes 8 | tf_op jit(solution)/shard_map/psum | solution.py:50
  363.3 0.1 slice.411
  363.4 1.3 collective-permute-start.6
  364.7 4.2 collective-permute-done.6
  368.9 4.6 %fusion.20 = f32[32,16]{0,1:T(8,128)S(1)} fusion(f32[32,16]{0,1:T(8,128)S(1)} %multiply_add_fusion.1, f32[7,16]{0,1:T(8,128)S(1)} %collective-permute-done.6, f32[]{:T(128)} %bitcast.8, f32[]{:T(128)} %bitcast.7, f32[]{:T(128)} %bitcast.6, f32[]{:T(128)} %bitcast.5, f32[]{:T(128)} %bitcast.4, f32[]{:T(128)} %bitcast.3, f32[]{:T(128)} %bitcast.2), kind=kLoop, calls=%fused_computation.34 | loop fusion | flops 10752 | bytes 4572 | tf_op jit(solution)/shard_map/sub | solution.py:20
  373.5 1.6 collective-permute-start.7
  375.2 17.6 %all_gather.23 = f32[32,256]{0,1:T(8,128)S(1)} all-gather(f32[32,16]{0,1:T(8,128)S(1)} %multiply_add_fusion.1), channel_id=1, replica_groups=mesh['day'=2,'stu'=16] {'stu'}, dimensions={1}, use_global_device_ids=true | all-gather | bytes 34816 | tf_op jit(solution)/shard_map/all_gather | solution.py:38
  392.8 5.3 %multiply_reduce_fusion = (f32[]{:T(128)}, f32[32,16]{0,1:T(8,128)S(1)}) fusion(f32[32,16]{0,1:T(8,128)S(1)} %multiply_add_fusion.1, f32[7,16]{0,1:T(8,128)S(1)} %collective-permute-done.7, f32[32,16]{0,1:T(8,128)S(1)} %fusion.20, f32[]{:T(128)} %bitcast.8, f32[]{:T(128)} %bitcast.7, f32[]{:T(128)} %bitcast.6, f32[]{:T(128)} %bitcast.5, f32[]{:T(128)} %bitcast.4, ...), kind=kOutput, calls=%fused_computation.227 | convolution fusion | flops 1585151 | bytes 55776 | tf_op jit(solution)/shard_map/dot_general | solution.py:37
  398.0 43.2 %psum.47 = f32[]{:T(128)} all-reduce(f32[]{:T(128)} %get-tuple-element.6), channel_id=1, replica_groups=mesh['day'=2,'stu'=16] {'day','stu'}, use_global_device_ids=true, to_apply=%region_14.0 | all-reduce | flops 1 | bytes 8 | tf_op jit(solution)/shard_map/psum | solution.py:50
  442.6 0.6 multiply_subtract_fusion
  (14 shorter events, 0.2 us)
Async XLA Ops:
  7.2 4.7 %copy-start = (bf16[1024,256]{1,0:T(8,128)(2,1)S(1)}, bf16[1024,256]{1,0:T(8,128)(2,1)}, u32[]{:S(2)}) copy-start(bf16[1024,256]{1,0:T(8,128)(2,1)} %param.7) | copy-start | bytes 1572868
  7.2 54.1 %all-gather.3.cloned.1.call-start = ((), (), s32[]{:S(2)}) async-start(), calls=%async_computation.2 | async-start | bytes 4456448 | tf_op jit(solution)/shard_map/all_gather | solution.py:54
  8.9 110.2 %reduce-scatter.2.cloned.1.call-start = ((), (), s32[]{:S(2)}) async-start(), calls=%async_computation.1 | async-start | bytes 139264 | tf_op jit(solution)/shard_map/reduce_scatter | solution.py:72
  9.9 21.7 %collective-permute-start = (f32[7,16]{0,1:T(8,128)S(1)}, f32[7,16]{0,1:T(8,128)S(1)}, u32[]{:S(2)}, u32[]{:S(2)}) collective-permute-start(f32[7,16]{0,1:T(8,128)S(1)} %slice.333), channel_id=1, source_target_pairs={{0,16},{1,17},{2,18},{3,19},{4,20},{5,21},{6,22},{7,23},{8,24},{9,... | collective-permute-start | bytes 1352 | tf_op jit(solution)/shard_map/ppermute | solution.py:14
  36.2 27.7 %collective-permute-start.1 = (f32[7,16]{0,1:T(8,128)S(1)}, f32[7,16]{0,1:T(8,128)S(1)}, u32[]{:S(2)}, u32[]{:S(2)}) collective-permute-start(f32[7,16]{0,1:T(8,128)S(1)} %bitcast.29), channel_id=1, source_target_pairs={{16,0},{17,1},{18,2},{19,3},{20,4},{21,5},{22,6},{23,7},{24,8},{25... | collective-permute-start | bytes 1352 | tf_op jit(solution)/shard_map/ppermute | solution.py:14
  124.6 5.5 %collective-permute-start.2 = (f32[7,16]{0,1:T(8,128)S(1)}, f32[7,16]{0,1:T(8,128)S(1)}, u32[]{:S(2)}, u32[]{:S(2)}) collective-permute-start(f32[7,16]{0,1:T(8,128)S(1)} %slice.359), channel_id=1, source_target_pairs={{0,16},{1,17},{2,18},{3,19},{4,20},{5,21},{6,22},{7,23},{8,24},{9,... | collective-permute-start | bytes 1352 | tf_op jit(solution)/shard_map/ppermute | solution.py:14
  134.7 17.0 %collective-permute-start.3 = (f32[7,16]{0,1:T(8,128)S(1)}, f32[7,16]{0,1:T(8,128)S(1)}, u32[]{:S(2)}, u32[]{:S(2)}) collective-permute-start(f32[7,16]{0,1:T(8,128)S(1)} %bitcast.31), channel_id=1, source_target_pairs={{16,0},{17,1},{18,2},{19,3},{20,4},{21,5},{22,6},{23,7},{24,8},{25... | collective-permute-start | bytes 1352 | tf_op jit(solution)/shard_map/ppermute | solution.py:14
  243.1 5.5 %collective-permute-start.4 = (f32[7,16]{0,1:T(8,128)S(1)}, f32[7,16]{0,1:T(8,128)S(1)}, u32[]{:S(2)}, u32[]{:S(2)}) collective-permute-start(f32[7,16]{0,1:T(8,128)S(1)} %slice.385), channel_id=1, source_target_pairs={{0,16},{1,17},{2,18},{3,19},{4,20},{5,21},{6,22},{7,23},{8,24},{9,... | collective-permute-start | bytes 1352 | tf_op jit(solution)/shard_map/ppermute | solution.py:14
  253.2 19.6 %collective-permute-start.5 = (f32[7,16]{0,1:T(8,128)S(1)}, f32[7,16]{0,1:T(8,128)S(1)}, u32[]{:S(2)}, u32[]{:S(2)}) collective-permute-start(f32[7,16]{0,1:T(8,128)S(1)} %bitcast.32), channel_id=1, source_target_pairs={{16,0},{17,1},{18,2},{19,3},{20,4},{21,5},{22,6},{23,7},{24,8},{25... | collective-permute-start | bytes 1352 | tf_op jit(solution)/shard_map/ppermute | solution.py:14
  363.4 5.5 %collective-permute-start.6 = (f32[7,16]{0,1:T(8,128)S(1)}, f32[7,16]{0,1:T(8,128)S(1)}, u32[]{:S(2)}, u32[]{:S(2)}) collective-permute-start(f32[7,16]{0,1:T(8,128)S(1)} %slice.411), channel_id=1, source_target_pairs={{0,16},{1,17},{2,18},{3,19},{4,20},{5,21},{6,22},{7,23},{8,24},{9,... | collective-permute-start | bytes 1352 | tf_op jit(solution)/shard_map/ppermute | solution.py:14
  373.5 19.3 %collective-permute-start.7 = (f32[7,16]{0,1:T(8,128)S(1)}, f32[7,16]{0,1:T(8,128)S(1)}, u32[]{:S(2)}, u32[]{:S(2)}) collective-permute-start(f32[7,16]{0,1:T(8,128)S(1)} %bitcast.30), channel_id=1, source_target_pairs={{16,0},{17,1},{18,2},{19,3},{20,4},{21,5},{22,6},{23,7},{24,8},{25... | collective-permute-start | bytes 1352 | tf_op jit(solution)/shard_map/ppermute | solution.py:14
Sparse Core Ops, SparseCore 0:
  10.2 51.0 all-gather.2
  64.7 54.3 reduce-scatter.1
